TPU v7x, 32 devices: a whole 2x2x4 slice. The times are simulated.
32 devices in a mesh: img: 8 (over z, y), band: 4 (over x, core).
Axes of the slice: x: 2, y: 2, z: 4, core: 2. Of those that a mesh axis runs over, the one named last changes fastest.
Arguments:
- patches: bfloat16 [32, 576, 768], P('img', 'band'), may hold values from -6 to 6
- patch_mask: int32 [32, 576], P('img', 'band'), may hold values from 0 to 1, as said below
- band_first: int32 [32, 4], P('img'), may hold values from 0 to 18, as said below
- attn_gain: bfloat16 [768], replicated, may hold values from 0.5 to 1.5
- attn_shift: bfloat16 [768], replicated, may hold values from -3 to 3
- inproj_weight: bfloat16 [768, 2304], replicated, may hold values from -0.21875 to 0.21875
- inproj_bias: bfloat16 [2304], replicated, may hold values from -2 to 2
- rotary_freqs: bfloat16 [2, 12, 32], replicated, may hold values from -3 to 3
- outproj_weight: bfloat16 [768, 768], replicated, may hold values from -0.875 to 0.875
- outproj_bias: bfloat16 [768], replicated, may hold values from -2 to 2
- mlp_gain: bfloat16 [768], replicated, may hold values from 0.5 to 1.5
- mlp_shift: bfloat16 [768], replicated, may hold values from -3 to 3
- expand_weight: bfloat16 [768, 3072], replicated, may hold values from -0.21875 to 0.21875
- expand_bias: bfloat16 [3072], replicated, may hold values from -2 to 2
- reduce_weight: bfloat16 [3072, 768], replicated, may hold values from -0.109375 to 0.109375
- reduce_bias: bfloat16 [768], replicated, may hold values from -2 to 2
- cotangent: bfloat16 [32, 576, 768], P('img', 'band'), may hold values from -6 to 6
Outputs:
- block_out: bfloat16 [32, 576, 768], P('img', 'band')
- d_patches: bfloat16 [32, 576, 768], P('img', 'band')
- grad_attn_gain: float32 [768], P('img')
- grad_attn_shift: float32 [768], P('img')
- grad_inproj_weight: float32 [768, 2304], P('img')
- grad_inproj_bias: float32 [2304], P('img')
- grad_rotary_freqs: float32 [2, 12, 32], replicated
- grad_outproj_weight: float32 [768, 768], P('img')
- grad_outproj_bias: float32 [768], P('img')
- grad_mlp_gain: float32 [768], P('img')
- grad_mlp_shift: float32 [768], P('img')
- grad_expand_weight: float32 [768, 3072], P('img')
- grad_expand_bias: float32 [3072], P('img')
- grad_reduce_weight: float32 [3072, 768], P('img')
- grad_reduce_bias: float32 [768], P('img')
Inputs may be any that keep to these rules, and one draw needn't show every extreme that they name: `patch_mask`: each image has a square grid of side 24 * 7 // 12, 20 or 24, and image 0 has side 24; the grid's rows are split over the 4 bands as evenly as possible, earlier bands taking one row more; a slot of local row i and column j of band b is 1 exactly when i is under the band's row count and j under the side. `band_first`: the first patch row of each band of each image, consistent with patch_mask's row counts.
All inputs are finite; a program needn't handle non-finite values.
Results may differ from a plain program's by a relative error of at most 0.012.
The roundings to bfloat16 on the way count: a program that leaves them out, or rounds other values in their place, can miss the bound.
Values may be sent and summed in bfloat16 or wider, within the bound.
No kernel may reach another device: no remote copies, remote signals or barrier semaphores. Data moves between devices by JAX's collectives and lax.ppermute only.
A program may use at most 192 MiB of HBM per device.

v0:
```python
import jax
import jax.numpy as jnp
from jax import lax
from jax.sharding import PartitionSpec as P

GRID = 24
EPS = 1e-06
NEG = -1e30


def norm_parts(values):
    center = values - jnp.mean(values, -1, keepdims=True)
    rstd = lax.rsqrt(jnp.mean(center * center, -1, keepdims=True) + EPS)
    return (center * rstd, rstd)


def norm_back(grad, gain, xhat, rstd):
    scaled = grad * gain
    inner = jnp.mean(scaled * xhat, -1, keepdims=True)
    return rstd * (scaled - jnp.mean(scaled, -1, keepdims=True) - xhat * inner)


def turn(tensor, cosine, sine):
    half = tensor.shape[-1] // 2
    first, second = (tensor[..., :half], tensor[..., half:])
    return jnp.concatenate([first * cosine - second * sine, first * sine + second * cosine], -1)


def matrix_sum(grad):
    low = grad.astype(jnp.bfloat16)
    low = lax.psum_scatter(low, "band", scatter_dimension=1, tiled=True)
    low = lax.psum_scatter(low, "img", scatter_dimension=0, tiled=True)
    low = lax.all_gather(low, "band", axis=1, tiled=True)
    return low.astype(jnp.float32)


def local(
    patches,
    patch_mask,
    band_first,
    attn_gain,
    attn_shift,
    inproj_weight,
    inproj_bias,
    rotary_freqs,
    outproj_weight,
    outproj_bias,
    mlp_gain,
    mlp_shift,
    expand_weight,
    expand_bias,
    reduce_weight,
    reduce_bias,
    cotangent,
):
    single = jnp.float32
    low = jnp.bfloat16
    images, slots, width = patches.shape
    heads = rotary_freqs.shape[1]
    size = width // heads
    scale = size ** (-0.5)
    bands = lax.axis_size("band")
    here = lax.axis_index("band")

    def gather_image(values):
        return lax.all_to_all(values, "band", 0, 1, tiled=True)

    def spread_image(values):
        return lax.all_to_all(values, "band", 1, 0, tiled=True)

    patches = gather_image(patches)
    cotangent = gather_image(cotangent)
    mask = gather_image(patch_mask).astype(single)
    count = images // bands
    total = slots * bands
    starts = lax.dynamic_slice_in_dim(band_first, here * count, count, 0)
    row_in = jnp.arange(slots) // GRID
    rows = (starts[:, :, None] + row_in[None, None, :]).reshape(count, total).astype(single)
    cols = jnp.broadcast_to((jnp.arange(total) % GRID).astype(single)[None, :], rows.shape)
    freqs = rotary_freqs.astype(single)
    angles = rows[..., None, None] * freqs[0] + cols[..., None, None] * freqs[1]
    cosine, sine = (jnp.cos(angles), jnp.sin(angles))
    wide = patches.astype(single)
    xhat_one, rstd_one = norm_parts(wide)
    gain_one = attn_gain.astype(single)
    attn_in = (xhat_one * gain_one + attn_shift.astype(single)).astype(low)
    projected = jnp.dot(attn_in, inproj_weight, preferred_element_type=single)
    projected = projected + inproj_bias.astype(single)
    split = projected.reshape(count, total, 3, heads, size)
    query_rot = turn(split[:, :, 0], cosine, sine).astype(low)
    key_rot = turn(split[:, :, 1], cosine, sine).astype(low)
    value_low = split[:, :, 2].astype(low)
    scores = jnp.einsum("iqhd,ikhd->ihqk", query_rot, key_rot, preferred_element_type=single)
    masked = jnp.where(mask[:, None, None, :] > 0, scores * scale, NEG)
    expo = jnp.exp(masked - jnp.max(masked, -1, keepdims=True))
    probs = expo / jnp.sum(expo, -1, keepdims=True)
    probs_low = probs.astype(low)
    mix = jnp.einsum("ihqk,ikhd->iqhd", probs_low, value_low, preferred_element_type=single)
    mix = mix.reshape(count, total, width).astype(low)
    attn_out = jnp.dot(mix, outproj_weight, preferred_element_type=single)
    resid_mid = wide + attn_out + outproj_bias.astype(single)
    xhat_two, rstd_two = norm_parts(resid_mid)
    gain_two = mlp_gain.astype(single)
    mlp_in = (xhat_two * gain_two + mlp_shift.astype(single)).astype(low)
    pre_act = jnp.dot(mlp_in, expand_weight, preferred_element_type=single)
    pre_act = pre_act + expand_bias.astype(single)
    half_erf = 0.5 + 0.5 * lax.erf(pre_act * 0.5**0.5)
    hidden = (pre_act * half_erf).astype(low)
    slope = half_erf + pre_act * jnp.exp(-0.5 * pre_act * pre_act) * 0.3989422804014327
    branch = jnp.dot(hidden, reduce_weight, preferred_element_type=single)
    block_out = mask[..., None] * (resid_mid + branch + reduce_bias.astype(single))
    block_out = spread_image(block_out.astype(low))
    grad_top = cotangent.astype(single) * mask[..., None]
    grad_low = grad_top.astype(low)
    grad_reduce_weight = jnp.einsum("iqf,iqd->fd", hidden, grad_low, preferred_element_type=single)
    grad_reduce_bias = jnp.sum(grad_top, (0, 1))
    d_hidden = jnp.einsum("iqd,fd->iqf", grad_low, reduce_weight, preferred_element_type=single)
    d_pre = (d_hidden * slope).astype(low)
    grad_expand_weight = jnp.einsum("iqd,iqf->df", mlp_in, d_pre, preferred_element_type=single)
    grad_expand_bias = jnp.sum(d_pre.astype(single), (0, 1))
    d_mlp_in = jnp.einsum("iqf,df->iqd", d_pre, expand_weight, preferred_element_type=single)
    grad_mlp_gain = jnp.sum(d_mlp_in * xhat_two, (0, 1))
    grad_mlp_shift = jnp.sum(d_mlp_in, (0, 1))
    d_mid = grad_top + norm_back(d_mlp_in, gain_two, xhat_two, rstd_two)
    d_attn = d_mid.astype(low)
    grad_outproj_weight = jnp.einsum("iqe,iqd->ed", mix, d_attn, preferred_element_type=single)
    grad_outproj_bias = jnp.sum(d_attn.astype(single), (0, 1))
    d_mix = jnp.einsum("iqd,ed->iqe", d_attn, outproj_weight, preferred_element_type=single)
    d_mix = d_mix.astype(low).reshape(count, total, heads, size)
    d_values = jnp.einsum("ihqk,iqhd->ikhd", probs_low, d_mix, preferred_element_type=single)
    d_probs = jnp.einsum("iqhd,ikhd->ihqk", d_mix, value_low, preferred_element_type=single)
    inner = jnp.sum(probs * d_probs, -1, keepdims=True)
    d_scores = (probs * (d_probs - inner)).astype(low)
    d_qrot = scale * jnp.einsum("ihqk,ikhd->iqhd", d_scores, key_rot, preferred_element_type=single)
    d_krot = scale * jnp.einsum(
        "ihqk,iqhd->ikhd", d_scores, query_rot, preferred_element_type=single
    )
    half = size // 2
    slope_q = (
        d_qrot[..., half:] * query_rot[..., :half] - d_qrot[..., :half] * query_rot[..., half:]
    )
    slope_k = d_krot[..., half:] * key_rot[..., :half] - d_krot[..., :half] * key_rot[..., half:]
    d_angle = slope_q + slope_k
    grad_freqs = jnp.stack(
        [
            jnp.sum(rows[..., None, None] * d_angle, (0, 1)),
            jnp.sum(cols[..., None, None] * d_angle, (0, 1)),
        ]
    )
    d_queries = turn(d_qrot, cosine, -sine)
    d_keys = turn(d_krot, cosine, -sine)
    flat = (count, total, width)
    d_proj = jnp.concatenate(
        [d_queries.reshape(flat), d_keys.reshape(flat), d_values.reshape(flat)], -1
    ).astype(low)
    grad_inproj_weight = jnp.einsum("iqd,iqe->de", attn_in, d_proj, preferred_element_type=single)
    grad_inproj_bias = jnp.sum(d_proj.astype(single), (0, 1))
    d_attn_in = jnp.einsum("iqe,de->iqd", d_proj, inproj_weight, preferred_element_type=single)
    grad_attn_gain = jnp.sum(d_attn_in * xhat_one, (0, 1))
    grad_attn_shift = jnp.sum(d_attn_in, (0, 1))
    d_patches = d_mid + norm_back(d_attn_in, gain_one, xhat_one, rstd_one)
    d_patches = spread_image(d_patches.astype(low))
    small = (
        grad_attn_gain,
        grad_attn_shift,
        grad_inproj_bias,
        grad_outproj_bias,
        grad_mlp_gain,
        grad_mlp_shift,
        grad_expand_bias,
        grad_reduce_bias,
        grad_freqs.reshape(-1),
    )
    packed = lax.psum(jnp.concatenate(small), ("img", "band"))
    shares = lax.axis_size("img")
    mine = lax.axis_index("img")
    sums = []
    at = 0
    for piece in small:
        long = piece.shape[0]
        sums.append(packed[at : at + long])
        at += long
    freq_total = sums.pop().reshape(grad_freqs.shape)
    sums = [
        lax.dynamic_slice_in_dim(s, mine * (s.shape[0] // shares), s.shape[0] // shares)
        for s in sums
    ]
    return (
        block_out,
        d_patches,
        sums[0],
        sums[1],
        matrix_sum(grad_inproj_weight),
        sums[2],
        freq_total,
        matrix_sum(grad_outproj_weight),
        sums[3],
        sums[4],
        sums[5],
        matrix_sum(grad_expand_weight),
        sums[6],
        matrix_sum(grad_reduce_weight),
        sums[7],
    )


def solution(mesh):
    act = P("img", "band", None)
    row = P("img")
    mat = P("img", None)
    return jax.shard_map(
        local,
        mesh=mesh,
        in_specs=(act, P("img", "band"), P("img", None)) + (P(),) * 13 + (act,),
        out_specs=(act, act, row, row, mat, row, P(), mat, row, row, row, mat, row, mat, row),
        check_vma=False,
    )
```

profile of v0, /device:TPU:0, one launch (start us, length us, event | category | flops | bytes accessed | tf_op | source)
XLA Modules:
  0.0 651.7 jit_solution(12072034389343736507)
XLA Ops:
  8.6 4.2 all-to-all-start
  16.7 4.2 all-to-all-start.1
  33.7 4.2 all-to-all-start.3
  45.8 4.6 convolution_add_fusion
  50.3 6.5 copy.68
  59.3 4.8 subtract_convert_fusion.1
  65.4 7.4 %fusion.34 = f32[12,576,576]{1,2,0:T(8,128)} fusion(bf16[576,12,32]{0,2,1:T(8,128)(2,1)S(1)} %bitcast.128, bf16[576,12,32]{0,2,1:T(8,128)(2,1)S(1)} %bitcast.130, bf16[576,12,32]{0,2,1:T(8,128)(2,1)S(1)} %bitcast.126, bf16[576,12,32]{0,2,1:T(8,128)(2,1)S(1)} %bitcast.124), kind=kOutput, calls=%fused_computation.88 | convolution fusion | flops 513146880 | bytes 17694720 | tf_op jit(solution)/shard_map/iqhd,ikhd->ihqk/dot_general | solution.py:93
  72.7 22.2 %fusion.54 = (f32[12,576]{1,0:T(8,128)}, f32[12,576,576]{1,2,0:T(8,128)}) fusion(f32[12,576,576]{1,2,0:T(8,128)} %fusion.34, pred[576]{0:T(1024)(128)(4,1)} %broadcast_compare_fusion), kind=kOutput, calls=%fused_computation.138 | output fusion | flops 23888448 | bytes 31878720 | tf_op jit(solution)/shard_map/sub | solution.py:95
  94.9 8.4 %fusion.21 = bf16[12,64,576]{2,1,0:T(8,128)(2,1)S(1)} fusion(f32[1,576,3,12,64]{1,4,3,2,0:T(8,128)} %bitcast.122, f32[12,576,576]{1,2,0:T(8,128)} %get-tuple-element.113, f32[12,576]{1,0:T(8,128)} %get-tuple-element.112), kind=kOutput, calls=%fused_computation.63 | convolution fusion | flops 518012928 | bytes 19603456 | tf_op jit(solution)/shard_map/ihqk,ikhd->iqhd/dot_general | solution.py:98
  104.2 3.3 fusion.20
  112.8 8.9 %multiply_convert_fusion.1 = (bf16[576,3072]{1,0:T(8,128)(2,1)}, f32[576,3072]{1,0:T(8,128)}) fusion(f32[3072]{0:T(1024)} %convert_element_type.313, bf16[768,3072]{1,0:T(8,128)(2,1)} %param.29, f32[576,768]{1,0:T(8,128)} %fusion.20, f32[768]{0:T(1024)} %convert_element_type.311, f32[768]{0:T(1024)} %convert_element_type.310, f32[576]{0:T(1024)S(1)} %add_rsqrt_fusion, ...), kind=kOutput, calls=%fused_computation.18 | convolution fusion | flops 2730737664 | bytes 17127936 | tf_op jit(solution)/shard_map/dot_general | solution.py:105
  123.2 9.2 %convert_reduce_fusion = (f32[3072]{0:T(1024)}, bf16[576,3072]{1,0:T(8,128)(2,1)S(1)}) fusion(f32[576,3072]{1,0:T(8,128)} %get-tuple-element.115, f32[3072]{0:T(1024)} %convert_element_type.313, bf16[576,768]{1,0:T(8,128)(2,1)S(1)} %fusion.19, bf16[3072,768]{1,0:T(8,128)(2,1)} %param.31), kind=kOutput, calls=%fused_computation.17 | convolution fusion | flops 2740909056 | bytes 16244736 | tf_op jit(solution)/shard_map/iqd,fd->iqf/dot_general | solution.py:117
  132.4 7.6 %multiply_reduce_fusion.1 = (f32[768]{0:T(1024)}, f32[576]{0:T(1024)S(1)}, f32[576]{0:T(1024)S(1)}, f32[768]{0:T(1024)}, f32[576,768]{1,0:T(8,128)S(1)}) fusion(f32[576,768]{1,0:T(8,128)S(1)} %copy-done.1, f32[576]{0:T(1024)S(1)} %copy-done.40, f32[576]{0:T(1024)S(1)} %copy-done.32, f32[768]{0:T(1024)S(1)} %copy-done.37, ...), kind=kOutput, calls=%fused_computation.46 | convolution fusion | flops 2721887744 | bytes 11814912 | tf_op jit(solution)/shard_map/iqf,df->iqd/dot_general | solution.py:121
  140.0 2.6 convert_reduce_fusion.2
  146.0 3.6 convolution_convert_fusion.4
  151.8 15.5 %multiply_reduce_fusion = (f32[12,576]{1,0:T(8,128)S(1)}, f32[12,576,576]{1,2,0:T(8,128)}) fusion(f32[12,576,576]{1,2,0:T(8,128)} %get-tuple-element.113, f32[12,576]{1,0:T(8,128)} %get-tuple-element.112, bf16[576,12,64]{0,2,1:T(8,128)(2,1)} %bitcast.144, f32[1,576,3,12,64]{1,4,3,2,0:T(8,128)} %bitcast.123), kind=kOutput, calls=%fused_computation.2 | convolution fusion | flops 521544960 | bytes 35654656 | tf_op jit(solution)/shard_map/iqhd,ikhd->ihqk/dot_general | solution.py:131
  167.3 12.5 %multiply_convert_fusion = bf16[12,576,576]{1,2,0:T(8,128)(2,1)S(1)} fusion(f32[12,576,576]{1,2,0:T(8,128)} %get-tuple-element.118, f32[12,576]{1,0:T(8,128)S(1)} %get-tuple-element.117, f32[12,576,576]{1,2,0:T(8,128)} %get-tuple-element.113, f32[12,576]{1,0:T(8,128)S(1)} %copy-done.27), kind=kLoop, calls=%fused_computation.1 | loop fusion | flops 15925248 | bytes 39868416 | tf_op jit(solution)/shard_map/convert_element_type | solution.py:133
  179.9 4.0 multiply_bitcast_fusion
  183.9 3.0 multiply_bitcast_fusion.1
  186.9 6.6 %multiply_subtract_fusion.1 = (bf16[1,576,12,32]{1,3,2,0:T(8,128)(2,1)S(1)}, bf16[1,576,12,32]{1,3,2,0:T(8,128)(2,1)S(1)}, bf16[1,576,12,32]{1,3,2,0:T(8,128)(2,1)S(1)}, bf16[1,576,12,32]{1,3,2,0:T(8,128)(2,1)S(1)}) fusion(f32[1,576,12,64]{1,3,2,0:T(8,128)} %multiply_bitcast_fusion.1, f32[12,32]{1,0:T(8,128)} %get-tuple-element.111, f32[576]{0:T(1024)S(1)} %copy-done.24, ...), kind=kLoop, calls=%fused_computation.78 | loop fusion | flops 4423680 | bytes 5316096 | tf_op jit(solution)/shard_map/sub | solution.py:26
  195.1 9.5 %fusion.24 = bf16[12,64,576]{2,1,0:T(8,128)(2,1)S(1)} fusion(bf16[576,12,64]{0,2,1:T(8,128)(2,1)S(1)} %bitcast.145, f32[12,576,576]{1,2,0:T(8,128)} %get-tuple-element.113, f32[12,576]{1,0:T(8,128)S(1)} %copy-done.28), kind=kOutput, calls=%fused_computation.64 | convolution fusion | flops 518012928 | bytes 17722368 | tf_op jit(solution)/shard_map/ihqk,iqhd->ikhd/dot_general | solution.py:130
  205.6 7.2 %convolution_convert_fusion = bf16[768,2304]{0,1:T(8,128)(2,1)} fusion(bf16[576,768]{0,1:T(8,128)(2,1)S(1)} %bitcast.146, bf16[576,768]{0,1:T(8,128)(2,1)S(1)} %bitcast.141, bf16[576,768]{0,1:T(8,128)(2,1)S(1)} %bitcast.138, f32[576,768]{1,0:T(8,128)S(1)} %copy-done.16, f32[768]{0:T(1024)S(1)} %copy-done.43, f32[768]{0:T(1024)S(1)} %copy-done.35), kind=kOutput, calls=%fused_computation.21 | convolution fusion | flops 2049490944 | bytes 7968768 | tf_op jit(solution)/shard_map/iqd,iqe->de/dot_general | solution.py:156
  213.0 8.3 %convolution_convert_fusion.1 = bf16[3072,768]{0,1:T(8,128)(2,1)} fusion(bf16[576,3072]{1,0:T(8,128)(2,1)} %get-tuple-element.114, bf16[576,768]{1,0:T(8,128)(2,1)} %copy-done.20), kind=kOutput, calls=%fused_computation.22 | convolution fusion | flops 2720268288 | bytes 9142272 | tf_op jit(solution)/shard_map/iqf,iqd->fd/dot_general | solution.py:115
  222.1 9.2 %convolution_convert_fusion.2 = bf16[768,3072]{1,0:T(8,128)(2,1)} fusion(bf16[576,3072]{1,0:T(8,128)(2,1)} %copy-done.50, f32[576,768]{1,0:T(8,128)} %fusion.20, f32[768]{0:T(1024)} %convert_element_type.311, f32[768]{0:T(1024)S(1)} %copy-done.38, f32[576]{0:T(1024)} %copy-done.39, f32[576]{0:T(1024)S(1)} %copy-done.33), kind=kOutput, calls=%fused_computation.23 | convolution fusion | flops 2722480128 | bytes 10037760 | tf_op jit(solution)/shard_map/iqd,iqf->df/dot_general | solution.py:119
  233.4 24.4 %reduce-scatter.15.cloned.1.call-done = bf16[768,576]{0,1:T(8,128)(2,1)} async-done(((bf16[768,2304]{0,1:T(8,128)(2,1)}), bf16[768,576]{0,1:T(8,128)(2,1)}) %reduce-scatter.15.cloned.1.call-update) | async-done | bytes 884752 | tf_op jit(solution)/shard_map/reduce_scatter | solution.py:31
  260.3 48.0 %reduce-scatter.23.cloned.1.call-done = bf16[3072,192]{0,1:T(8,128)(2,1)} async-done(((bf16[3072,768]{0,1:T(8,128)(2,1)}), bf16[3072,192]{0,1:T(8,128)(2,1)}) %reduce-scatter.23.cloned.1.call-update) | async-done | bytes 1179664 | tf_op jit(solution)/shard_map/reduce_scatter | solution.py:31
  310.8 6.8 %fusion.27 = bf16[1,576,768]{2,1,0:T(8,128)(2,1)S(1)} fusion(f32[576,768]{1,0:T(8,128)} %fusion.20, bf16[576,3072]{1,0:T(8,128)(2,1)} %get-tuple-element.114, bf16[3072,768]{1,0:T(8,128)(2,1)} %param.31, f32[768]{0:T(1024)S(1)} %convert_element_type.315, f32[576]{0:T(1024)S(1)} %convert_element_type.290), kind=kOutput, calls=%fused_computation.67 | convolution fusion | flops 2719678464 | bytes 10917120 | tf_op jit(solution)/shard_map/dot_general | solution.py:110
  320.8 8.0 %reduce.39 = bf16[576,768]{1,0:T(8,128)(2,1)} reduce(bf16[576,1,768]{2,1,0:T(2,128)(2,1)} %bitcast.134, bf16[]{:T(256)} %broadcast.353), dimensions={1}, to_apply=%bitcast.118.reduce_sub_computation | reduce | bytes 1769474
  328.8 3.5 reshape.788
  332.3 4.2 all-to-all-start.2
  336.8 6.8 %fusion.52 = (f32[768]{0:T(1024)S(1)}, f32[768]{0:T(1024)S(1)}, f32[576]{0:T(1024)S(1)}, f32[576]{0:T(1024)S(1)}, f32[576,768]{1,0:T(8,128)}) fusion(f32[576]{0:T(1024)S(1)} %copy-done.30, f32[576]{0:T(1024)S(1)} %copy-done.23, bf16[4,144,768]{2,1,0:T(8,128)(2,1)} %all-to-all-done.1, f32[576,768]{1,0:T(8,128)} %copy-done.15, ...), kind=kOutput, calls=%fused_computation.136 | convolution fusion | flops 2050815488 | bytes 10635264 | tf_op jit(solution)/shard_map/iqe,de->iqd/dot_general | solution.py:158
  348.6 19.5 %reduce-scatter.19.cloned.1.call-done = bf16[768,768]{1,0:T(8,128)(2,1)} async-done(((bf16[768,3072]{1,0:T(8,128)(2,1)}), bf16[768,768]{1,0:T(8,128)(2,1)}) %reduce-scatter.19.cloned.1.call-update) | async-done | bytes 1179664 | tf_op jit(solution)/shard_map/reduce_scatter | solution.py:31
  369.4 2.9 fusion.33
  376.2 7.9 %reduce.40 = bf16[576,768]{1,0:T(8,128)(2,1)} reduce(bf16[576,1,768]{2,1,0:T(2,128)(2,1)} %bitcast.135, bf16[]{:T(256)} %broadcast.353), dimensions={1}, to_apply=%bitcast.117.reduce_sub_computation | reduce | bytes 1769474
  384.1 3.4 reshape.790
  390.1 3.3 multiply_reduce_fusion.9
  394.0 4.5 all-to-all-start.4
  404.8 41.6 %psum.7 = f32[10752]{0:T(1024)} all-reduce(f32[10752]{0:T(1024)} %constant_dynamic-update-slice_fusion), channel_id=1, replica_groups=mesh['img'=8,'band'=4] {'img','band'}, use_global_device_ids=true, to_apply=%region_21.22 | all-reduce | flops 10752 | bytes 86016 | tf_op jit(solution)/shard_map/psum | solution.py:174
  458.0 3.8 reshape.789
  464.3 3.8 reshape.791
  472.2 7.9 %all_gather.13 = bf16[96,768]{0,1:T(8,128)(2,1)} all-gather(bf16[96,192]{0,1:T(8,128)(2,1)} %copy.89), channel_id=1, replica_groups=mesh['img'=8,'band'=4] {'band'}, dimensions={1}, use_global_device_ids=true | all-gather | bytes 184320 | tf_op jit(solution)/shard_map/all_gather | solution.py:33
  481.9 18.5 %reduce-scatter.25.cloned.1.call-done = bf16[96,576]{1,0:T(8,128)(2,1)} async-done(((bf16[768,576]{1,0:T(8,128)(2,1)}), bf16[96,576]{1,0:T(8,128)(2,1)}) %reduce-scatter.25.cloned.1.call-update) | async-done | bytes 110608
  503.8 7.2 %all-gather = bf16[4,576,96]{1,2,0:T(8,128)(2,1)S(1)} all-gather(bf16[1,576,96]{1,2,0:T(8,128)(2,1)} %copy.77), channel_id=1, replica_groups=mesh['img'=8,'band'=4] {'band'}, dimensions={0}, use_global_device_ids=true | all-gather | bytes 552960 | tf_op jit(solution)/shard_map/all_gather | solution.py:33
  512.2 2.7 reshape.779
  514.9 53.6 %reduce-scatter.29.cloned.1.call-done = bf16[384,192]{1,0:T(8,128)(2,1)} async-done(((bf16[3072,192]{1,0:T(8,128)(2,1)}), bf16[384,192]{1,0:T(8,128)(2,1)}) %reduce-scatter.29.cloned.1.call-update) | async-done | bytes 147472
  570.2 8.4 %all_gather.15 = bf16[384,768]{0,1:T(8,128)(2,1)} all-gather(bf16[384,192]{0,1:T(8,128)(2,1)} %copy.91), channel_id=1, replica_groups=mesh['img'=8,'band'=4] {'band'}, dimensions={1}, use_global_device_ids=true | all-gather | bytes 737280 | tf_op jit(solution)/shard_map/all_gather | solution.py:33
  580.8 54.7 %reduce-scatter.21.cloned.1.call-done = bf16[96,768]{1,0:T(8,128)(2,1)} async-done(((bf16[768,768]{1,0:T(8,128)(2,1)}), bf16[96,768]{1,0:T(8,128)(2,1)}) %reduce-scatter.21.cloned.1.call-update) | async-done | bytes 147472 | tf_op jit(solution)/shard_map/reduce_scatter | solution.py:32
  635.5 7.7 %all_gather.14 = bf16[96,3072]{1,0:T(8,128)(2,1)S(1)} all-gather(bf16[96,768]{1,0:T(8,128)(2,1)} %reduce-scatter.21.cloned.1.call-done), channel_id=1, replica_groups=mesh['img'=8,'band'=4] {'band'}, dimensions={1}, use_global_device_ids=true | all-gather | bytes 737280 | tf_op jit(solution)/shard_map/all_gather | solution.py:33
  (211 shorter events, 105.9 us)
Async XLA Ops:
  7.2 38.6 %copy-start = (bf16[768,2304]{1,0:T(8,128)(2,1)S(1)}, bf16[768,2304]{1,0:T(8,128)(2,1)}, u32[]{:S(2)}) copy-start(bf16[768,2304]{1,0:T(8,128)(2,1)} %param.22) | copy-start | bytes 10616836
  8.6 8.0 %all-to-all-start = ((s32[4,1,144]{2,1,0:T(1,128)}), s32[4,1,144]{2,1,0:T(1,128)S(1)}, u32[]{:S(2)}, u32[]{:S(2)}) async-start(s32[4,1,144]{2,1,0:T(1,128)} %all_to_all.17), calls=%async_computation | async-start | bytes 8192 | tf_op jit(solution)/shard_map/all_to_all | solution.py:66
  16.7 17.0 %all-to-all-start.1 = ((bf16[4,144,768]{2,1,0:T(8,128)(2,1)}), bf16[4,144,768]{2,1,0:T(8,128)(2,1)}, u32[]{:S(2)}, u32[]{:S(2)}) async-start(bf16[4,144,768]{2,1,0:T(8,128)(2,1)} %param.17), calls=%async_computation.1 | async-start | bytes 1769472 | tf_op jit(solution)/shard_map/all_to_all | solution.py:66
  33.7 88.0 %all-to-all-start.3 = ((bf16[4,144,768]{2,1,0:T(8,128)(2,1)}), bf16[4,144,768]{2,1,0:T(8,128)(2,1)}, u32[]{:S(2)}, u32[]{:S(2)}) async-start(bf16[4,144,768]{2,1,0:T(8,128)(2,1)} %param.33), calls=%async_computation.3 | async-start | bytes 1769472 | tf_op jit(solution)/shard_map/all_to_all | solution.py:66
  37.9 193.4 %reduce-scatter.17.cloned.1.call-start = ((), (), s32[]{:S(2)}) async-start(), calls=%async_computation.14 | async-start | bytes 1474560 | tf_op jit(solution)/shard_map/reduce_scatter | solution.py:31
  42.1 3.7 copy-start.34
  42.1 3.7 copy-start.41
  42.1 3.7 copy-start.42
  56.8 2.4 copy-start.21
  56.8 2.4 copy-start.24
  56.9 2.4 copy-start.25
  94.9 9.3 %copy-start.44 = (f32[768]{0:T(1024)S(1)}, f32[768]{0:T(1024)}, u32[]{:S(2)}) copy-start(f32[768]{0:T(1024)} %convert_element_type.309) | copy-start | bytes 9220
  94.9 9.3 %copy-start.47 = (bf16[768,768]{1,0:T(8,128)(2,1)S(1)}, bf16[768,768]{1,0:T(8,128)(2,1)}, u32[]{:S(2)}) copy-start(bf16[768,768]{1,0:T(8,128)(2,1)} %param.25) | copy-start | bytes 3538948
  123.1 9.2 %copy-start.20 = (bf16[576,768]{1,0:T(8,128)(2,1)}, bf16[576,768]{1,0:T(8,128)(2,1)S(1)}, u32[]{:S(2)}) copy-start(bf16[576,768]{1,0:T(8,128)(2,1)S(1)} %fusion.19) | copy-start | bytes 2654212
  123.1 9.2 %copy-start.1 = (f32[576,768]{1,0:T(8,128)S(1)}, f32[576,768]{1,0:T(8,128)}, u32[]{:S(2)}) copy-start(f32[576,768]{1,0:T(8,128)} %fusion.20) | copy-start | bytes 5308420
  123.1 9.2 %copy-start.32 = (f32[576]{0:T(1024)S(1)}, f32[576]{0:T(1024)}, u32[]{:S(2)}) copy-start(f32[576]{0:T(1024)} %copy-done.31) | copy-start | bytes 6916
  123.1 9.2 %copy-start.37 = (f32[768]{0:T(1024)S(1)}, f32[768]{0:T(1024)}, u32[]{:S(2)}) copy-start(f32[768]{0:T(1024)} %convert_element_type.310) | copy-start | bytes 9220
  123.2 9.2 %copy-start.40 = (f32[576]{0:T(1024)S(1)}, f32[576]{0:T(1024)}, u32[]{:S(2)}) copy-start(f32[576]{0:T(1024)} %copy-done.39) | copy-start | bytes 6916
  132.4 7.6 %copy-start.50 = (bf16[576,3072]{1,0:T(8,128)(2,1)}, bf16[576,3072]{1,0:T(8,128)(2,1)S(1)}, u32[]{:S(2)}) copy-start(bf16[576,3072]{1,0:T(8,128)(2,1)S(1)} %get-tuple-element.121) | copy-start | bytes 10616836
  140.0 3.8 copy-start.49
  151.8 15.5 %copy-start.27 = (f32[12,576]{1,0:T(8,128)S(1)}, f32[12,576]{1,0:T(8,128)}, u32[]{:S(2)}) copy-start(f32[12,576]{1,0:T(8,128)} %get-tuple-element.112) | copy-start | bytes 82948
  167.3 12.5 %copy-start.3 = (bf16[1,576,12,32]{1,3,2,0:T(8,128)(2,1)S(1)}, bf16[1,576,12,32]{1,3,2,0:T(8,128)(2,1)}, u32[]{:S(2)}) copy-start(bf16[1,576,12,32]{1,3,2,0:T(8,128)(2,1)} %copy-done.2) | copy-start | bytes 1327108
  167.3 12.6 %copy-start.5 = (bf16[1,576,12,32]{1,3,2,0:T(8,128)(2,1)S(1)}, bf16[1,576,12,32]{1,3,2,0:T(8,128)(2,1)}, u32[]{:S(2)}) copy-start(bf16[1,576,12,32]{1,3,2,0:T(8,128)(2,1)} %copy-done.4) | copy-start | bytes 1327108
  179.8 4.0 copy-start.7
  179.9 4.0 copy-start.9
  186.9 70.9 %reduce-scatter.15.cloned.1.call-start = ((), (), s32[]{:S(2)}) async-start(), calls=%async_computation.13 | async-start | bytes 4423680 | tf_op jit(solution)/shard_map/reduce_scatter | solution.py:31
  193.6 11.0 %copy-start.11 = (bf16[1,576,12,64]{1,3,2,0:T(8,128)(2,1)}, bf16[1,576,12,64]{1,3,2,0:T(8,128)(2,1)S(1)}, u32[]{:S(2)}) copy-start(bf16[1,576,12,64]{1,3,2,0:T(8,128)(2,1)S(1)} %maximum_convert_fusion) | copy-start | bytes 2654212
  195.1 9.5 %copy-start.13 = (bf16[1,576,12,64]{1,3,2,0:T(8,128)(2,1)}, bf16[1,576,12,64]{1,3,2,0:T(8,128)(2,1)S(1)}, u32[]{:S(2)}) copy-start(bf16[1,576,12,64]{1,3,2,0:T(8,128)(2,1)S(1)} %maximum_convert_fusion.1) | copy-start | bytes 2654212
  195.1 10.5 %copy-start.16 = (f32[576,768]{1,0:T(8,128)S(1)}, f32[576,768]{1,0:T(8,128)}, u32[]{:S(2)}) copy-start(f32[576,768]{1,0:T(8,128)} %copy-done.15) | copy-start | bytes 5308420
  195.1 10.5 %copy-start.35 = (f32[768]{0:T(1024)S(1)}, f32[768]{0:T(1024)}, u32[]{:S(2)}) copy-start(f32[768]{0:T(1024)} %convert_element_type.296) | copy-start | bytes 9220
  195.1 10.4 %copy-start.43 = (f32[768]{0:T(1024)S(1)}, f32[768]{0:T(1024)}, u32[]{:S(2)}) copy-start(f32[768]{0:T(1024)} %convert_element_type.297) | copy-start | bytes 9220
  212.8 95.5 %reduce-scatter.23.cloned.1.call-start = ((), (), s32[]{:S(2)}) async-start(), calls=%async_computation.17 | async-start | bytes 5898240 | tf_op jit(solution)/shard_map/reduce_scatter | solution.py:31
  221.4 146.7 %reduce-scatter.19.cloned.1.call-start = ((), (), s32[]{:S(2)}) async-start(), calls=%async_computation.15 | async-start | bytes 5898240 | tf_op jit(solution)/shard_map/reduce_scatter | solution.py:31
  231.3 29.0 %copy-start.46 = (bf16[768]{0:T(1024)(128)(2,1)S(1)}, bf16[768]{0:T(1024)(128)(2,1)}, u32[]{:S(2)}) copy-start(bf16[768]{0:T(1024)(128)(2,1)} %param.32) | copy-start | bytes 4612
  231.3 239.4 %reduce-scatter.27.cloned.1.call-start = ((), (), s32[]{:S(2)}) async-start(), calls=%async_computation.19 | async-start | bytes 442368
  233.3 267.1 %reduce-scatter.25.cloned.1.call-start = ((), (), s32[]{:S(2)}) async-start(), calls=%async_computation.18 | async-start | bytes 1105920
  260.0 308.4 %reduce-scatter.29.cloned.1.call-start = ((), (), s32[]{:S(2)}) async-start(), calls=%async_computation.20 | async-start | bytes 1769472
  328.8 8.0 %copy-start.23 = (f32[576]{0:T(1024)S(1)}, f32[576]{0:T(1024)}, u32[]{:S(2)}) copy-start(f32[576]{0:T(1024)} %copy-done.22) | copy-start | bytes 6916
  328.8 8.0 %copy-start.30 = (f32[576]{0:T(1024)S(1)}, f32[576]{0:T(1024)}, u32[]{:S(2)}) copy-start(f32[576]{0:T(1024)} %copy-done.29) | copy-start | bytes 6916
  332.3 61.7 %all-to-all-start.2 = ((bf16[4,2,55296]{2,1,0:T(2,128)(2,1)}), bf16[4,2,55296]{2,1,0:T(2,128)(2,1)}, u32[]{:S(2)}, u32[]{:S(2)}) async-start(bf16[4,2,55296]{2,1,0:T(2,128)(2,1)} %reshape.788), calls=%async_computation.2 | async-start | bytes 1769472 | tf_op jit(solution)/shard_map/all_to_all | solution.py:69
  336.5 299.0 %reduce-scatter.21.cloned.1.call-start = ((), (), s32[]{:S(2)}) async-start(), calls=%async_computation.16 | async-start | bytes 1327104 | tf_op jit(solution)/shard_map/reduce_scatter | solution.py:32
  336.8 9.4 %copy-start.12 = (bf16[1,576,12,64]{1,3,2,0:T(8,128)(2,1)S(1)}, bf16[1,576,12,64]{1,3,2,0:T(8,128)(2,1)}, u32[]{:S(2)}) copy-start(bf16[1,576,12,64]{1,3,2,0:T(8,128)(2,1)} %copy-done.11) | copy-start | bytes 2654212
  336.8 9.4 %copy-start.14 = (bf16[1,576,12,64]{1,3,2,0:T(8,128)(2,1)S(1)}, bf16[1,576,12,64]{1,3,2,0:T(8,128)(2,1)}, u32[]{:S(2)}) copy-start(bf16[1,576,12,64]{1,3,2,0:T(8,128)(2,1)} %copy-done.13) | copy-start | bytes 2654212
  336.8 9.4 %copy-start.19 = (bf16[12,64,576]{2,1,0:T(8,128)(2,1)S(1)}, bf16[12,64,576]{2,1,0:T(8,128)(2,1)}, u32[]{:S(2)}) copy-start(bf16[12,64,576]{2,1,0:T(8,128)(2,1)} %copy-done.18) | copy-start | bytes 2654212
  369.4 2.9 copy-start.36
  376.2 12.6 %copy-start.45 = (f32[768]{0:T(1024)S(1)}, f32[768]{0:T(1024)}, u32[]{:S(2)}) copy-start(f32[768]{0:T(1024)} %get-tuple-element.80) | copy-start | bytes 9220
  376.2 13.9 %copy-start.26 = (f32[576]{0:T(1024)S(1)}, f32[576]{0:T(1024)}, u32[]{:S(2)}) copy-start(f32[576]{0:T(1024)} %get-tuple-element.123) | copy-start | bytes 6916
  394.0 70.3 %all-to-all-start.4 = ((bf16[4,2,55296]{2,1,0:T(2,128)(2,1)}), bf16[4,2,55296]{2,1,0:T(2,128)(2,1)}, u32[]{:S(2)}, u32[]{:S(2)}) async-start(bf16[4,2,55296]{2,1,0:T(2,128)(2,1)} %reshape.790), calls=%async_computation.4 | async-start | bytes 1769472 | tf_op jit(solution)/shard_map/all_to_all | solution.py:69
  (16 other events, 17.6 us)
Sparse Core Ops, SparseCore 0:
  187.0 27.7 reduce-scatter.16
  217.4 40.3 reduce-scatter.14
  260.3 47.9 reduce-scatter.22
  310.7 57.2 reduce-scatter.18
  371.1 62.2 reduce-scatter.26
  437.2 63.1 reduce-scatter.24
  503.8 64.5 reduce-scatter.28
  571.9 63.6 reduce-scatter.20
where the time goes:
time: 658 us; the launch traced here: 652 us
  waiting for transfers between devices  220 us (33%)
  matrix products  125 us (19%)
  other arithmetic  99.8 us (15%)
  local copies, waits for them, and re-layouts  95.8 us (15%)
  blocking collectives  72.8 us (11%)
  starting transfers between devices  22.4 us (3%)
  between operations  15.3 us (2%)
    reduce_scatter x4, waiting for transfers between devices, matrix_sum(): low = lax.psum_scatter(low, 'band', scatter_dimension=1, tiled=True)  91.9 us
    unnamed x11, waiting for transfers between devices  72.2 us
    unnamed x127, local copies, waits for them, and re-layouts  57.3 us
    reduce_scatter x1, waiting for transfers between devices, matrix_sum(): low = lax.psum_scatter(low, 'img', scatter_dimension=0, tiled=True)  54.7 us
    psum x1, blocking collectives, local(): packed = lax.psum(jnp.concatenate(small), ('img', 'band'))  41.6 us
    all_gather x4, blocking collectives, matrix_sum(): low = lax.all_gather(low, 'band', axis=1, tiled=True)  31.2 us
    sub x1, other arithmetic, local(): expo = jnp.exp(masked - jnp.max(masked, -1, keepdims=True))  22.2 us
    unnamed x3, other arithmetic  16 us
  transfers between devices with their start and end apart: 13, of which 7 were waited for; matrix products, arithmetic and copies ran while one was open for 38% of the time, Pallas kernels for 0%

commit v1 on v0

--- a/solution.py
+++ b/solution.py
@@ -8,6 +8,23 @@
 NEG = -1e30
 
 
+def in_order(tiles, dim):
+    lengths = list(tiles.shape[1:])
+    lengths[dim] *= tiles.shape[0]
+    return jnp.moveaxis(tiles, 0, dim).reshape(lengths)
+
+
+def doubled(x, axis):
+    devices, here = (lax.axis_size(axis), lax.axis_index(axis))
+    tiles, bit = (x[None], 1)
+    while bit < devices:
+        theirs = lax.ppermute(tiles, axis, [(i, i ^ bit) for i in range(devices)])
+        low = here & bit == 0
+        tiles = jnp.concatenate([jnp.where(low, tiles, theirs), jnp.where(low, theirs, tiles)])
+        bit *= 2
+    return tiles
+
+
 def norm_parts(values):
     center = values - jnp.mean(values, -1, keepdims=True)
     rstd = lax.rsqrt(jnp.mean(center * center, -1, keepdims=True) + EPS)
@@ -30,7 +47,7 @@
     low = grad.astype(jnp.bfloat16)
     low = lax.psum_scatter(low, "band", scatter_dimension=1, tiled=True)
     low = lax.psum_scatter(low, "img", scatter_dimension=0, tiled=True)
-    low = lax.all_gather(low, "band", axis=1, tiled=True)
+    low = in_order(doubled(low, "band"), 1)
     return low.astype(jnp.float32)
 
 

time: 658 us -> 669 us (1.017)
  blocking collectives: 72.8 us -> 41.8 us
  waiting for transfers between devices: 220 us -> 248 us
  other arithmetic: 99.8 us -> 109 us
    all_gather x4 -> x0, blocking collectives: 31.2 us -> none  [matrix_sum(): low = lax.all_gather(low, 'band', axis=1, tiled=True)]
    unnamed x11, waiting for transfers between devices: 72.2 us -> 91.6 us
    ppermute x0 -> x8, waiting for transfers between devices: none -> 8.36 us  [doubled(): theirs = lax.ppermute(tiles, axis, [(i, i ^ bit) for i in range(devices)])]
    select_n x0 -> x8, other arithmetic: none -> 7.54 us  [doubled(): jnp.where(low, tiles, theirs)]
    unnamed x127 -> x159, local copies, waits for them, and re-layouts: 57.3 us -> 60 us
    unnamed x3 -> x4, other arithmetic: 16 us -> 16.1 us
  transfers between devices with their start and end apart: 13 -> 21, of which waited for: 7 -> 10; matrix products, arithmetic and copies ran while one was open for 38% -> 38% of each run, Pallas kernels for 0% -> 0%
where the time goes in v1:
time: 669 us; the launch traced here: 662 us
  waiting for transfers between devices  248 us (37%)
  matrix products  124 us (19%)
  other arithmetic  109 us (16%)
  local copies, waits for them, and re-layouts  96.9 us (14%)
  blocking collectives  41.8 us (6%)
  starting transfers between devices  26.6 us (4%)
  between operations  15.5 us (2%)
    unnamed x11, waiting for transfers between devices  91.6 us
    reduce_scatter x4, waiting for transfers between devices, matrix_sum(): low = lax.psum_scatter(low, 'band', scatter_dimension=1, tiled=True)  86.3 us
    reduce_scatter x1, waiting for transfers between devices, matrix_sum(): low = lax.psum_scatter(low, 'img', scatter_dimension=0, tiled=True)  60.5 us
    unnamed x159, local copies, waits for them, and re-layouts  60 us
    psum x1, blocking collectives, local(): packed = lax.psum(jnp.concatenate(small), ('img', 'band'))  41.8 us
    sub x1, other arithmetic, local(): expo = jnp.exp(masked - jnp.max(masked, -1, keepdims=True))  22.3 us
    unnamed x4, other arithmetic  16.1 us
    dot_general x1, matrix products, local(): jnp.einsum('iqhd,ikhd->ihqk', d_mix, value_low, preferred_element_type=si...  15.5 us
  transfers between devices with their start and end apart: 21, of which 10 were waited for; matrix products, arithmetic and copies ran while one was open for 38% of the time, Pallas kernels for 0%

profile of v1, /device:TPU:0, one launch (start us, length us, event | category | flops | bytes accessed | tf_op | source)
XLA Modules:
  0.0 662.2 jit_solution(3951728900937166714)
XLA Ops:
  8.6 4.2 all-to-all-start
  16.7 4.2 all-to-all-start.1
  33.7 4.2 all-to-all-start.3
  45.7 4.6 convolution_add_fusion
  50.3 6.5 copy.70
  59.3 4.8 subtract_convert_fusion.1
  65.3 7.4 %fusion.34 = f32[12,576,576]{1,2,0:T(8,128)} fusion(bf16[576,12,32]{0,2,1:T(8,128)(2,1)S(1)} %bitcast.147, bf16[576,12,32]{0,2,1:T(8,128)(2,1)S(1)} %bitcast.149, bf16[576,12,32]{0,2,1:T(8,128)(2,1)S(1)} %bitcast.145, bf16[576,12,32]{0,2,1:T(8,128)(2,1)S(1)} %bitcast.143), kind=kOutput, calls=%fused_computation.89 | convolution fusion | flops 513146880 | bytes 17694720 | tf_op jit(solution)/shard_map/iqhd,ikhd->ihqk/dot_general | solution.py:110
  72.7 22.3 %fusion.54 = (f32[12,576]{1,0:T(8,128)}, f32[12,576,576]{1,2,0:T(8,128)}) fusion(f32[12,576,576]{1,2,0:T(8,128)} %fusion.34, pred[576]{0:T(1024)(128)(4,1)} %broadcast_compare_fusion), kind=kOutput, calls=%fused_computation.162 | output fusion | flops 23888448 | bytes 31878720 | tf_op jit(solution)/shard_map/sub | solution.py:112
  95.1 8.4 %fusion.21 = bf16[12,64,576]{2,1,0:T(8,128)(2,1)S(1)} fusion(f32[1,576,3,12,64]{1,4,3,2,0:T(8,128)} %bitcast.141, f32[12,576,576]{1,2,0:T(8,128)} %get-tuple-element.129, f32[12,576]{1,0:T(8,128)} %get-tuple-element.128), kind=kOutput, calls=%fused_computation.63 | convolution fusion | flops 518012928 | bytes 19603456 | tf_op jit(solution)/shard_map/ihqk,ikhd->iqhd/dot_general | solution.py:115
  104.4 3.3 fusion.20
  113.0 8.9 %multiply_convert_fusion.1 = (bf16[576,3072]{1,0:T(8,128)(2,1)}, f32[576,3072]{1,0:T(8,128)}) fusion(f32[3072]{0:T(1024)} %convert_element_type.337, bf16[768,3072]{1,0:T(8,128)(2,1)} %param.29, f32[576,768]{1,0:T(8,128)} %fusion.20, f32[768]{0:T(1024)} %convert_element_type.335, f32[768]{0:T(1024)} %convert_element_type.334, f32[576]{0:T(1024)S(1)} %add_rsqrt_fusion, ...), kind=kOutput, calls=%fused_computation.18 | convolution fusion | flops 2730737664 | bytes 17127936 | tf_op jit(solution)/shard_map/dot_general | solution.py:122
  123.3 9.2 %convert_reduce_fusion = (f32[3072]{0:T(1024)}, bf16[576,3072]{1,0:T(8,128)(2,1)S(1)}) fusion(f32[576,3072]{1,0:T(8,128)} %get-tuple-element.131, f32[3072]{0:T(1024)} %convert_element_type.337, bf16[576,768]{1,0:T(8,128)(2,1)S(1)} %fusion.19, bf16[3072,768]{1,0:T(8,128)(2,1)} %param.31), kind=kOutput, calls=%fused_computation.17 | convolution fusion | flops 2740909056 | bytes 16244736 | tf_op jit(solution)/shard_map/iqd,fd->iqf/dot_general | solution.py:134
  132.5 7.6 %multiply_reduce_fusion.1 = (f32[768]{0:T(1024)}, f32[576]{0:T(1024)S(1)}, f32[576]{0:T(1024)S(1)}, f32[768]{0:T(1024)}, f32[576,768]{1,0:T(8,128)S(1)}) fusion(f32[576,768]{1,0:T(8,128)S(1)} %copy-done.3, f32[576]{0:T(1024)S(1)} %copy-done.55, f32[576]{0:T(1024)S(1)} %copy-done.45, f32[768]{0:T(1024)S(1)} %copy-done.52, ...), kind=kOutput, calls=%fused_computation.46 | convolution fusion | flops 2721887744 | bytes 11814912 | tf_op jit(solution)/shard_map/iqf,df->iqd/dot_general | solution.py:138
  140.2 2.6 convert_reduce_fusion.2
  146.1 3.6 convolution_convert_fusion.4
  152.0 15.5 %multiply_reduce_fusion = (f32[12,576]{1,0:T(8,128)S(1)}, f32[12,576,576]{1,2,0:T(8,128)}) fusion(f32[12,576,576]{1,2,0:T(8,128)} %get-tuple-element.129, f32[12,576]{1,0:T(8,128)} %get-tuple-element.128, bf16[576,12,64]{0,2,1:T(8,128)(2,1)} %bitcast.167, f32[1,576,3,12,64]{1,4,3,2,0:T(8,128)} %bitcast.142), kind=kOutput, calls=%fused_computation.2 | convolution fusion | flops 521544960 | bytes 35654656 | tf_op jit(solution)/shard_map/iqhd,ikhd->ihqk/dot_general | solution.py:148
  167.5 12.5 %multiply_convert_fusion = bf16[12,576,576]{1,2,0:T(8,128)(2,1)S(1)} fusion(f32[12,576,576]{1,2,0:T(8,128)} %get-tuple-element.134, f32[12,576]{1,0:T(8,128)S(1)} %get-tuple-element.133, f32[12,576,576]{1,2,0:T(8,128)} %get-tuple-element.129, f32[12,576]{1,0:T(8,128)S(1)} %copy-done.39), kind=kLoop, calls=%fused_computation.1 | loop fusion | flops 15925248 | bytes 39868416 | tf_op jit(solution)/shard_map/convert_element_type | solution.py:150
  180.1 4.0 multiply_bitcast_fusion
  184.0 3.0 multiply_bitcast_fusion.1
  187.1 6.6 multiply_subtract_fusion.1
  195.3 9.5 %fusion.24 = bf16[12,64,576]{2,1,0:T(8,128)(2,1)S(1)} fusion(bf16[576,12,64]{0,2,1:T(8,128)(2,1)S(1)} %bitcast.168, f32[12,576,576]{1,2,0:T(8,128)} %get-tuple-element.129, f32[12,576]{1,0:T(8,128)S(1)} %copy-done.40), kind=kOutput, calls=%fused_computation.64 | convolution fusion | flops 518012928 | bytes 17722368 | tf_op jit(solution)/shard_map/ihqk,iqhd->ikhd/dot_general | solution.py:147
  205.7 7.3 %convolution_convert_fusion = bf16[768,2304]{0,1:T(8,128)(2,1)} fusion(bf16[576,768]{0,1:T(8,128)(2,1)S(1)} %bitcast.169, bf16[576,768]{0,1:T(8,128)(2,1)S(1)} %bitcast.162, bf16[576,768]{0,1:T(8,128)(2,1)S(1)} %bitcast.159, f32[576,768]{1,0:T(8,128)S(1)} %copy-done.23, f32[768]{0:T(1024)S(1)} %copy-done.58, f32[768]{0:T(1024)S(1)} %copy-done.49), kind=kOutput, calls=%fused_computation.21 | convolution fusion | flops 2049490944 | bytes 7968768 | tf_op jit(solution)/shard_map/iqd,iqe->de/dot_general | solution.py:173
  213.3 8.3 %convolution_convert_fusion.1 = bf16[3072,768]{0,1:T(8,128)(2,1)} fusion(bf16[576,3072]{1,0:T(8,128)(2,1)} %get-tuple-element.130, bf16[576,768]{1,0:T(8,128)(2,1)} %copy-done.31), kind=kOutput, calls=%fused_computation.22 | convolution fusion | flops 2720268288 | bytes 9142272 | tf_op jit(solution)/shard_map/iqf,iqd->fd/dot_general | solution.py:132
  222.3 9.2 %convolution_convert_fusion.2 = bf16[768,3072]{1,0:T(8,128)(2,1)} fusion(bf16[576,3072]{1,0:T(8,128)(2,1)} %copy-done.66, f32[576,768]{1,0:T(8,128)} %fusion.20, f32[768]{0:T(1024)} %convert_element_type.335, f32[768]{0:T(1024)S(1)} %copy-done.53, f32[576]{0:T(1024)} %copy-done.54, f32[576]{0:T(1024)S(1)} %copy-done.46), kind=kOutput, calls=%fused_computation.23 | convolution fusion | flops 2722480128 | bytes 10037760 | tf_op jit(solution)/shard_map/iqd,iqf->df/dot_general | solution.py:136
  233.8 24.2 %reduce-scatter.15.cloned.1.call-done = bf16[768,576]{0,1:T(8,128)(2,1)} async-done(((bf16[768,2304]{0,1:T(8,128)(2,1)}), bf16[768,576]{0,1:T(8,128)(2,1)}) %reduce-scatter.15.cloned.1.call-update) | async-done | bytes 884752 | tf_op jit(solution)/shard_map/reduce_scatter | solution.py:48
  260.2 6.8 %fusion.27 = bf16[1,576,768]{2,1,0:T(8,128)(2,1)S(1)} fusion(f32[576,768]{1,0:T(8,128)} %fusion.20, bf16[576,3072]{1,0:T(8,128)(2,1)} %get-tuple-element.130, bf16[3072,768]{1,0:T(8,128)(2,1)} %param.31, f32[768]{0:T(1024)S(1)} %convert_element_type.339, f32[576]{0:T(1024)S(1)} %convert_element_type.314), kind=kOutput, calls=%fused_computation.67 | convolution fusion | flops 2719678464 | bytes 10917120 | tf_op jit(solution)/shard_map/dot_general | solution.py:127
  267.1 2.6 copy.101
  270.1 8.1 %reduce.39 = bf16[576,768]{1,0:T(8,128)(2,1)} reduce(bf16[576,1,768]{2,1,0:T(2,128)(2,1)} %bitcast.153, bf16[]{:T(256)} %broadcast.357), dimensions={1}, to_apply=%bitcast.137.reduce_sub_computation | reduce | bytes 1769474
  278.2 3.4 reshape.801
  281.6 4.2 all-to-all-start.2
  285.9 32.0 %reduce-scatter.23.cloned.1.call-done = bf16[3072,192]{0,1:T(8,128)(2,1)} async-done(((bf16[3072,768]{0,1:T(8,128)(2,1)}), bf16[3072,192]{0,1:T(8,128)(2,1)}) %reduce-scatter.23.cloned.1.call-update) | async-done | bytes 1179664 | tf_op jit(solution)/shard_map/reduce_scatter | solution.py:48
  318.0 2.5 copy.92
  320.9 5.9 fusion.52
  335.5 2.7 fusion.33
  338.2 30.0 %reduce-scatter.19.cloned.1.call-done = bf16[768,768]{1,0:T(8,128)(2,1)} async-done(((bf16[768,3072]{1,0:T(8,128)(2,1)}), bf16[768,768]{1,0:T(8,128)(2,1)}) %reduce-scatter.19.cloned.1.call-update) | async-done | bytes 1179664 | tf_op jit(solution)/shard_map/reduce_scatter | solution.py:48
  369.6 3.8 copy.100
  373.3 7.9 %reduce.40 = bf16[576,768]{1,0:T(8,128)(2,1)} reduce(bf16[576,1,768]{2,1,0:T(2,128)(2,1)} %bitcast.154, bf16[]{:T(256)} %broadcast.357), dimensions={1}, to_apply=%bitcast.136.reduce_sub_computation | reduce | bytes 1769474
  381.3 3.4 reshape.803
  386.0 4.5 all-to-all-start.4
  396.7 41.8 %psum.7 = f32[10752]{0:T(1024)} all-reduce(f32[10752]{0:T(1024)} %constant_dynamic-update-slice_fusion), channel_id=1, replica_groups=mesh['img'=8,'band'=4] {'img','band'}, use_global_device_ids=true, to_apply=%region_21.22 | all-reduce | flops 10752 | bytes 86016 | tf_op jit(solution)/shard_map/psum | solution.py:191
  451.6 3.8 reshape.802
  455.4 2.5 copy.94
  457.9 3.8 reshape.804
  465.7 34.8 %reduce-scatter.25.cloned.1.call-done = bf16[96,576]{1,0:T(8,128)(2,1)} async-done(((bf16[768,576]{1,0:T(8,128)(2,1)}), bf16[96,576]{1,0:T(8,128)(2,1)}) %reduce-scatter.25.cloned.1.call-update) | async-done | bytes 110608
  511.9 56.6 %reduce-scatter.29.cloned.1.call-done = bf16[384,192]{1,0:T(8,128)(2,1)} async-done(((bf16[3072,192]{1,0:T(8,128)(2,1)}), bf16[384,192]{1,0:T(8,128)(2,1)}) %reduce-scatter.29.cloned.1.call-update) | async-done | bytes 147472
  575.1 60.5 %reduce-scatter.21.cloned.1.call-done = bf16[96,768]{1,0:T(8,128)(2,1)} async-done(((bf16[768,768]{1,0:T(8,128)(2,1)}), bf16[96,768]{1,0:T(8,128)(2,1)}) %reduce-scatter.21.cloned.1.call-update) | async-done | bytes 147472 | tf_op jit(solution)/shard_map/reduce_scatter | solution.py:49
  641.1 5.5 collective-permute-done.7
  647.7 2.7 copy.83
  (269 shorter events, 115.0 us)
Async XLA Ops:
  7.2 38.5 %copy-start = (bf16[768,2304]{1,0:T(8,128)(2,1)S(1)}, bf16[768,2304]{1,0:T(8,128)(2,1)}, u32[]{:S(2)}) copy-start(bf16[768,2304]{1,0:T(8,128)(2,1)} %param.22) | copy-start | bytes 10616836
  8.6 8.0 %all-to-all-start = ((s32[4,1,144]{2,1,0:T(1,128)}), s32[4,1,144]{2,1,0:T(1,128)S(1)}, u32[]{:S(2)}, u32[]{:S(2)}) async-start(s32[4,1,144]{2,1,0:T(1,128)} %all_to_all.17), calls=%async_computation | async-start | bytes 8192 | tf_op jit(solution)/shard_map/all_to_all | solution.py:83
  16.7 17.0 %all-to-all-start.1 = ((bf16[4,144,768]{2,1,0:T(8,128)(2,1)}), bf16[4,144,768]{2,1,0:T(8,128)(2,1)}, u32[]{:S(2)}, u32[]{:S(2)}) async-start(bf16[4,144,768]{2,1,0:T(8,128)(2,1)} %param.17), calls=%async_computation.1 | async-start | bytes 1769472 | tf_op jit(solution)/shard_map/all_to_all | solution.py:83
  33.7 88.2 %all-to-all-start.3 = ((bf16[4,144,768]{2,1,0:T(8,128)(2,1)}), bf16[4,144,768]{2,1,0:T(8,128)(2,1)}, u32[]{:S(2)}, u32[]{:S(2)}) async-start(bf16[4,144,768]{2,1,0:T(8,128)(2,1)} %param.33), calls=%async_computation.3 | async-start | bytes 1769472 | tf_op jit(solution)/shard_map/all_to_all | solution.py:83
  37.9 193.7 %reduce-scatter.17.cloned.1.call-start = ((), (), s32[]{:S(2)}) async-start(), calls=%async_computation.14 | async-start | bytes 1474560 | tf_op jit(solution)/shard_map/reduce_scatter | solution.py:48
  95.1 9.3 %copy-start.59 = (f32[768]{0:T(1024)S(1)}, f32[768]{0:T(1024)}, u32[]{:S(2)}) copy-start(f32[768]{0:T(1024)} %convert_element_type.333) | copy-start | bytes 9220
  95.1 9.3 %copy-start.63 = (bf16[768,768]{1,0:T(8,128)(2,1)S(1)}, bf16[768,768]{1,0:T(8,128)(2,1)}, u32[]{:S(2)}) copy-start(bf16[768,768]{1,0:T(8,128)(2,1)} %param.25) | copy-start | bytes 3538948
  123.3 9.2 %copy-start.31 = (bf16[576,768]{1,0:T(8,128)(2,1)}, bf16[576,768]{1,0:T(8,128)(2,1)S(1)}, u32[]{:S(2)}) copy-start(bf16[576,768]{1,0:T(8,128)(2,1)S(1)} %fusion.19) | copy-start | bytes 2654212
  123.3 9.2 %copy-start.3 = (f32[576,768]{1,0:T(8,128)S(1)}, f32[576,768]{1,0:T(8,128)}, u32[]{:S(2)}) copy-start(f32[576,768]{1,0:T(8,128)} %fusion.20) | copy-start | bytes 5308420
  123.3 9.2 %copy-start.45 = (f32[576]{0:T(1024)S(1)}, f32[576]{0:T(1024)}, u32[]{:S(2)}) copy-start(f32[576]{0:T(1024)} %copy-done.44) | copy-start | bytes 6916
  123.3 9.2 %copy-start.52 = (f32[768]{0:T(1024)S(1)}, f32[768]{0:T(1024)}, u32[]{:S(2)}) copy-start(f32[768]{0:T(1024)} %convert_element_type.334) | copy-start | bytes 9220
  123.3 9.2 %copy-start.55 = (f32[576]{0:T(1024)S(1)}, f32[576]{0:T(1024)}, u32[]{:S(2)}) copy-start(f32[576]{0:T(1024)} %copy-done.54) | copy-start | bytes 6916
  152.0 15.5 %copy-start.39 = (f32[12,576]{1,0:T(8,128)S(1)}, f32[12,576]{1,0:T(8,128)}, u32[]{:S(2)}) copy-start(f32[12,576]{1,0:T(8,128)} %get-tuple-element.128) | copy-start | bytes 82948
  167.5 12.5 %copy-start.5 = (bf16[1,576,12,32]{1,3,2,0:T(8,128)(2,1)S(1)}, bf16[1,576,12,32]{1,3,2,0:T(8,128)(2,1)}, u32[]{:S(2)}) copy-start(bf16[1,576,12,32]{1,3,2,0:T(8,128)(2,1)} %copy-done.4) | copy-start | bytes 1327108
  167.5 12.6 %copy-start.8 = (bf16[1,576,12,32]{1,3,2,0:T(8,128)(2,1)S(1)}, bf16[1,576,12,32]{1,3,2,0:T(8,128)(2,1)}, u32[]{:S(2)}) copy-start(bf16[1,576,12,32]{1,3,2,0:T(8,128)(2,1)} %copy-done.7) | copy-start | bytes 1327108
  187.0 70.9 %reduce-scatter.15.cloned.1.call-start = ((), (), s32[]{:S(2)}) async-start(), calls=%async_computation.13 | async-start | bytes 4423680 | tf_op jit(solution)/shard_map/reduce_scatter | solution.py:48
  193.8 11.0 %copy-start.18 = (bf16[1,576,12,64]{1,3,2,0:T(8,128)(2,1)}, bf16[1,576,12,64]{1,3,2,0:T(8,128)(2,1)S(1)}, u32[]{:S(2)}) copy-start(bf16[1,576,12,64]{1,3,2,0:T(8,128)(2,1)S(1)} %maximum_convert_fusion) | copy-start | bytes 2654212
  195.3 9.5 %copy-start.20 = (bf16[1,576,12,64]{1,3,2,0:T(8,128)(2,1)}, bf16[1,576,12,64]{1,3,2,0:T(8,128)(2,1)S(1)}, u32[]{:S(2)}) copy-start(bf16[1,576,12,64]{1,3,2,0:T(8,128)(2,1)S(1)} %maximum_convert_fusion.1) | copy-start | bytes 2654212
  195.3 10.4 %copy-start.23 = (f32[576,768]{1,0:T(8,128)S(1)}, f32[576,768]{1,0:T(8,128)}, u32[]{:S(2)}) copy-start(f32[576,768]{1,0:T(8,128)} %copy-done.22) | copy-start | bytes 5308420
  195.3 10.4 %copy-start.49 = (f32[768]{0:T(1024)S(1)}, f32[768]{0:T(1024)}, u32[]{:S(2)}) copy-start(f32[768]{0:T(1024)} %convert_element_type.320) | copy-start | bytes 9220
  195.3 10.4 %copy-start.58 = (f32[768]{0:T(1024)S(1)}, f32[768]{0:T(1024)}, u32[]{:S(2)}) copy-start(f32[768]{0:T(1024)} %convert_element_type.321) | copy-start | bytes 9220
  213.0 104.9 %reduce-scatter.23.cloned.1.call-start = ((), (), s32[]{:S(2)}) async-start(), calls=%async_computation.17 | async-start | bytes 5898240 | tf_op jit(solution)/shard_map/reduce_scatter | solution.py:48
  221.6 146.6 %reduce-scatter.19.cloned.1.call-start = ((), (), s32[]{:S(2)}) async-start(), calls=%async_computation.15 | async-start | bytes 5898240 | tf_op jit(solution)/shard_map/reduce_scatter | solution.py:48
  231.5 28.7 %copy-start.62 = (bf16[768]{0:T(1024)(128)(2,1)S(1)}, bf16[768]{0:T(1024)(128)(2,1)}, u32[]{:S(2)}) copy-start(bf16[768]{0:T(1024)(128)(2,1)} %param.32) | copy-start | bytes 4612
  231.5 207.0 %reduce-scatter.27.cloned.1.call-start = ((), (), s32[]{:S(2)}) async-start(), calls=%async_computation.19 | async-start | bytes 442368
  233.5 267.1 %reduce-scatter.25.cloned.1.call-start = ((), (), s32[]{:S(2)}) async-start(), calls=%async_computation.18 | async-start | bytes 1105920
  281.6 104.3 %all-to-all-start.2 = ((bf16[4,2,55296]{2,1,0:T(2,128)(2,1)}), bf16[4,2,55296]{2,1,0:T(2,128)(2,1)}, u32[]{:S(2)}, u32[]{:S(2)}) async-start(bf16[4,2,55296]{2,1,0:T(2,128)(2,1)} %reshape.801), calls=%async_computation.2 | async-start | bytes 1769472 | tf_op jit(solution)/shard_map/all_to_all | solution.py:86
  285.9 35.0 %copy-start.35 = (f32[576]{0:T(1024)S(1)}, f32[576]{0:T(1024)}, u32[]{:S(2)}) copy-start(f32[576]{0:T(1024)} %copy-done.34) | copy-start | bytes 6916
  285.9 35.0 %copy-start.42 = (f32[576]{0:T(1024)S(1)}, f32[576]{0:T(1024)}, u32[]{:S(2)}) copy-start(f32[576]{0:T(1024)} %copy-done.41) | copy-start | bytes 6916
  285.9 282.6 %reduce-scatter.29.cloned.1.call-start = ((), (), s32[]{:S(2)}) async-start(), calls=%async_computation.20 | async-start | bytes 1769472
  320.5 315.0 %reduce-scatter.21.cloned.1.call-start = ((), (), s32[]{:S(2)}) async-start(), calls=%async_computation.16 | async-start | bytes 1327104 | tf_op jit(solution)/shard_map/reduce_scatter | solution.py:49
  320.9 8.7 %copy-start.19 = (bf16[1,576,12,64]{1,3,2,0:T(8,128)(2,1)S(1)}, bf16[1,576,12,64]{1,3,2,0:T(8,128)(2,1)}, u32[]{:S(2)}) copy-start(bf16[1,576,12,64]{1,3,2,0:T(8,128)(2,1)} %copy-done.18) | copy-start | bytes 2654212
  320.9 8.7 %copy-start.21 = (bf16[1,576,12,64]{1,3,2,0:T(8,128)(2,1)S(1)}, bf16[1,576,12,64]{1,3,2,0:T(8,128)(2,1)}, u32[]{:S(2)}) copy-start(bf16[1,576,12,64]{1,3,2,0:T(8,128)(2,1)} %copy-done.20) | copy-start | bytes 2654212
  320.9 8.7 %copy-start.30 = (bf16[12,64,576]{2,1,0:T(8,128)(2,1)S(1)}, bf16[12,64,576]{2,1,0:T(8,128)(2,1)}, u32[]{:S(2)}) copy-start(bf16[12,64,576]{2,1,0:T(8,128)(2,1)} %copy-done.29) | copy-start | bytes 2654212
  320.9 11.9 %copy-start.2 = (f32[1,576,12,64]{1,3,2,0:T(8,128)S(1)}, f32[1,576,12,64]{1,3,2,0:T(8,128)}, u32[]{:S(2)}) copy-start(f32[1,576,12,64]{1,3,2,0:T(8,128)} %multiply_bitcast_fusion.1) | copy-start | bytes 5308420
  320.9 11.9 %copy-start.12 = (bf16[1,576,12,32]{1,3,2,0:T(8,128)(2,1)S(1)}, bf16[1,576,12,32]{1,3,2,0:T(8,128)(2,1)}, u32[]{:S(2)}) copy-start(bf16[1,576,12,32]{1,3,2,0:T(8,128)(2,1)} %copy-done.10) | copy-start | bytes 1327108
  320.9 11.9 %copy-start.15 = (bf16[1,576,12,32]{1,3,2,0:T(8,128)(2,1)S(1)}, bf16[1,576,12,32]{1,3,2,0:T(8,128)(2,1)}, u32[]{:S(2)}) copy-start(bf16[1,576,12,32]{1,3,2,0:T(8,128)(2,1)} %copy-done.13) | copy-start | bytes 1327108
  335.5 32.8 %copy-start.60 = (f32[768]{0:T(1024)S(1)}, f32[768]{0:T(1024)}, u32[]{:S(2)}) copy-start(f32[768]{0:T(1024)} %get-tuple-element.80) | copy-start | bytes 9220
  373.3 11.3 %copy-start.47 = (f32[12,32]{1,0:T(8,128)S(1)}, f32[12,32]{1,0:T(8,128)}, u32[]{:S(2)}) copy-start(f32[12,32]{1,0:T(8,128)} %get-tuple-element.85) | copy-start | bytes 4612
  386.0 72.0 %all-to-all-start.4 = ((bf16[4,2,55296]{2,1,0:T(2,128)(2,1)}), bf16[4,2,55296]{2,1,0:T(2,128)(2,1)}, u32[]{:S(2)}, u32[]{:S(2)}) async-start(bf16[4,2,55296]{2,1,0:T(2,128)(2,1)} %reshape.803), calls=%async_computation.4 | async-start | bytes 1769472 | tf_op jit(solution)/shard_map/all_to_all | solution.py:86
  440.0 24.3 %collective-permute-start.2 = (bf16[1,96,192]{1,2,0:T(8,128)(2,1)}, bf16[1,96,192]{1,2,0:T(8,128)(2,1)}, u32[]{:S(2)}, u32[]{:S(2)}) collective-permute-start(bf16[1,96,192]{1,2,0:T(8,128)(2,1)} %bitcast.176), channel_id=1, source_target_pairs={{0,1},{1,0},{2,3},{3,2},{4,5},{5,4},{6,7},{7,6},{8,9},{9,8},{10,11... | collective-permute-start | bytes 110600 | tf_op jit(solution)/shard_map/ppermute | solution.py:21
  502.2 2.4 collective-permute-start
  503.1 5.3 collective-permute-start.3
  507.0 63.2 %collective-permute-start.1 = (bf16[2,96,576]{1,2,0:T(8,128)(2,1)}, bf16[2,96,576]{1,2,0:T(8,128)(2,1)}, u32[]{:S(2)}, u32[]{:S(2)}) collective-permute-start(bf16[2,96,576]{1,2,0:T(8,128)(2,1)} %pad_maximum_fusion.9), channel_id=1, source_target_pairs={{0,2},{1,3},{2,0},{3,1},{4,6},{5,7},{6,4},{7,5},{8,10},{9,11},{10,... | collective-permute-start | bytes 663560 | tf_op jit(solution)/shard_map/ppermute | solution.py:21
  570.2 65.3 %collective-permute-start.6 = (bf16[1,384,192]{1,2,0:T(8,128)(2,1)}, bf16[1,384,192]{1,2,0:T(8,128)(2,1)}, u32[]{:S(2)}, u32[]{:S(2)}) collective-permute-start(bf16[1,384,192]{1,2,0:T(8,128)(2,1)} %bitcast.175), channel_id=1, source_target_pairs={{0,1},{1,0},{2,3},{3,2},{4,5},{5,4},{6,7},{7,6},{8,9},{9,8},{10,11... | collective-permute-start | bytes 442376 | tf_op jit(solution)/shard_map/ppermute | solution.py:21
  635.5 2.6 collective-permute-start.4
  636.6 9.9 %collective-permute-start.7 = (bf16[2,384,192]{1,2,0:T(8,128)(2,1)S(1)}, bf16[2,384,192]{1,2,0:T(8,128)(2,1)S(1)}, u32[]{:S(2)}, u32[]{:S(2)}) collective-permute-start(bf16[2,384,192]{1,2,0:T(8,128)(2,1)S(1)} %pad_maximum_fusion.11), channel_id=1, source_target_pairs={{0,2},{1,3},{2,0},{3,1},{4,6},{5,7},{6,4},{7,5},{8,10},{9,11},{10,... | collective-permute-start | bytes 884744 | tf_op jit(solution)/shard_map/ppermute | solution.py:21
  640.5 12.0 %collective-permute-start.5 = (bf16[2,96,768]{2,1,0:T(8,128)(2,1)}, bf16[2,96,768]{2,1,0:T(8,128)(2,1)}, u32[]{:S(2)}, u32[]{:S(2)}) collective-permute-start(bf16[2,96,768]{2,1,0:T(8,128)(2,1)} %pad_maximum_fusion.10), channel_id=1, source_target_pairs={{0,2},{1,3},{2,0},{3,1},{4,6},{5,7},{6,4},{7,5},{8,10},{9,11},{10,... | collective-permute-start | bytes 884744 | tf_op jit(solution)/shard_map/ppermute | solution.py:21
  (40 other events, 99.9 us)
Sparse Core Ops, SparseCore 0:
  187.1 27.8 reduce-scatter.16
  217.6 40.3 reduce-scatter.14
  260.5 57.4 reduce-scatter.22
  320.4 47.8 reduce-scatter.18
  371.3 62.2 reduce-scatter.26
  437.4 63.1 reduce-scatter.24
  504.0 64.4 reduce-scatter.28
  571.9 63.6 reduce-scatter.20
